TPU v7x, 32 devices: a whole 2x2x4 slice. The times are simulated.
32 devices in a mesh: rows: 8 (over z, y), dims: 4 (over x, core).
Axes of the slice: x: 2, y: 2, z: 4, core: 2. Of those that a mesh axis runs over, the one named last changes fastest.
Arguments:
- table: bfloat16 [1, 256, 32768], P(None, 'dims', 'rows'), may hold values from -6 to 6
- accum: float32 [1, 32768], P(None, 'rows'), may hold values from 0.5 to 8
- grad_pooled: bfloat16 [1, 256, 1024], P(None, 'dims', 'rows'), may hold values from -6 to 6
- sample_slot: int32 [1, 8, 8, 1280], P(None, 'rows'), may hold values from 0 to 127
- row_slot: int32 [1, 8, 8, 1280], P(None, 'rows'), may hold values from 0 to 4095
- weight: int32 [1, 8, 8, 1280], P(None, 'rows'), may hold values from 1 to 3
- send_count: int32 [1, 8, 8], P(None, 'rows'), may hold values from 1 to 1280, as said below
Outputs:
- pooled: float32 [1, 256, 1024], P(None, 'dims', 'rows')
- new_table: bfloat16 [1, 256, 32768], P(None, 'dims', 'rows')
- new_accum: float32 [1, 32768], P(None, 'rows')
Inputs may be any that keep to these rules, and one draw needn't show every extreme that they name: `send_count`: at most 1280 live entries from one row shard to one owner per feature; in every feature one owner receives exactly 1280 from every row shard. Slots at or after the count are unused.
All inputs are finite; a program needn't handle non-finite values.
Results may differ from a plain program's by a relative error of at most 0.001.
Values may be sent and summed in bfloat16 or wider, within the bound.
No kernel may reach another device: no remote copies, remote signals or barrier semaphores. Data moves between devices by JAX's collectives and lax.ppermute only.
A program may use at most 64 MiB of HBM per device.

v0:
```python
import math
import jax
import jax.numpy as jnp
from jax import lax
from jax.sharding import PartitionSpec as P

D = 256
step_size = 0.3


def shards(table, accum, grad_pooled, sample_slot, row_slot, weight, send_count):
    feat_count, dim_local, row_local = table.shape
    peer_count = lax.axis_size("rows")
    own_samples = grad_pooled.shape[2]
    slot_count = sample_slot.shape[3]
    entry_count = peer_count * slot_count
    block_rows = math.gcd(row_local, 512)
    block_count = row_local // block_rows
    sample_local = sample_slot.reshape(feat_count, peer_count, slot_count)
    row_index = row_slot.reshape(feat_count, peer_count, slot_count)
    flat_rows = row_index.reshape(feat_count, 1, entry_count)
    live_count = send_count.reshape(feat_count, peer_count)
    slot_iota = lax.broadcasted_iota(jnp.int32, (1, 1, slot_count), 2)
    live_mask = slot_iota < live_count[:, :, None]
    weights = jnp.where(live_mask, weight.reshape(feat_count, peer_count, slot_count), 0)
    flat_weights = weights.reshape(feat_count, 1, entry_count).astype(jnp.bfloat16)
    block_iota = lax.broadcasted_iota(jnp.int32, (1, block_rows, 1), 1)

    def lookup_block(carry, block):
        start = block * block_rows
        table_part = lax.dynamic_slice_in_dim(table, start, block_rows, 2)
        selector = (flat_rows == block_iota + start).astype(jnp.bfloat16)
        return (
            carry
            + jnp.einsum("fdr,fre->fde", table_part, selector, preferred_element_type=jnp.float32),
            None,
        )

    looked_up, _ = lax.scan(
        lookup_block,
        jnp.zeros((feat_count, dim_local, entry_count), jnp.float32),
        jnp.arange(block_count, dtype=jnp.int32),
    )
    picked = looked_up.astype(jnp.bfloat16).reshape(feat_count, dim_local, peer_count, slot_count)
    positions = lax.broadcasted_iota(jnp.int32, (1, 1, 1, own_samples), 3)
    onehot = jnp.where(sample_local[..., None] == positions, weights[..., None], 0).astype(
        jnp.bfloat16
    )
    pooled = lax.psum_scatter(
        jnp.einsum("fdnk,fnkj->nfdj", picked, onehot, preferred_element_type=jnp.float32),
        "rows",
        scatter_dimension=0,
        tiled=True,
    ).reshape(feat_count, dim_local, own_samples)
    all_grads = lax.all_gather(grad_pooled, "rows", axis=2, tiled=True)
    all_grads = all_grads.reshape(feat_count, dim_local, peer_count, own_samples)
    selector = (sample_local[..., None] == positions).astype(jnp.bfloat16)
    entry_values = jnp.einsum(
        "fdnj,fnkj->fdnk", all_grads, selector, preferred_element_type=jnp.float32
    ).astype(jnp.bfloat16)
    entry_flat = entry_values.reshape(feat_count, dim_local, entry_count)

    def gradient_block(block):
        start = block * block_rows
        weighted = jnp.where(flat_rows == block_iota + start, flat_weights, 0)
        return jnp.einsum("fde,fre->fdr", entry_flat, weighted, preferred_element_type=jnp.float32)

    grad_blocks = lax.map(gradient_block, jnp.arange(block_count, dtype=jnp.int32))
    row_grad = jnp.moveaxis(grad_blocks, 0, 2).reshape(feat_count, dim_local, row_local)
    squares = jnp.sum(row_grad * row_grad, axis=1)
    norm_total = lax.psum(squares, "dims")
    new_accum = accum + norm_total / D
    new_table = (
        table.astype(jnp.float32) - step_size * row_grad / jnp.sqrt(new_accum)[:, None, :]
    ).astype(jnp.bfloat16)
    return (pooled, new_table, new_accum)


def solution(mesh):
    return jax.shard_map(
        shards,
        mesh=mesh,
        in_specs=(
            P(None, "dims", "rows"),
            P(None, "rows"),
            P(None, "dims", "rows"),
            P(None, "rows", None, None),
            P(None, "rows", None, None),
            P(None, "rows", None, None),
            P(None, "rows", None),
        ),
        out_specs=(P(None, "dims", "rows"), P(None, "dims", "rows"), P(None, "rows")),
        check_vma=False,
    )
```

profile of v0, /device:TPU:0, one launch (start us, length us, event | category | flops | bytes accessed | tf_op | source)
XLA Modules:
  0.0 151.7 jit_solution(12816893557992294160)
XLA Ops:
  7.2 0.8 reshape_reshape.3
  8.1 48.6 %while.25 = (s32[]{:T(128)}, f32[1,64,10240]{2,1,0:T(8,128)S(1)}, s32[8]{0:T(128)S(1)}, bf16[1,64,4096]{2,1,0:T(8,128)(2,1)}, s32[1,1,10240]{2,1,0:T(1,128)S(1)}...) while((s32[]{:T(128)}, f32[1,64,10240]{2,1,0:T(8,128)S(1)}, s32[8]{0:T(128)S(1)}, ...), condition=%wide.region_1.2_spmd.clone, body=%wide.region_0.1_spmd.clone.sunk | while | flops 677642752 | bytes 5353649 | solution.py:39
  8.1 0.6 dynamic_slice.25
  9.3 4.8 %fusion.55 = f32[1,64,10240]{2,1,0:T(8,128)S(1)} fusion(s32[10240]{0:T(1024)S(1)} %bitcast.90, s32[512]{0:T(512)S(1)} %bitcast.88, f32[1,64,10240]{2,1,0:T(8,128)S(1)} %get-tuple-element.264, pred[]{:T(512)S(6)} %compare.3, bf16[1,64,4096]{2,1,0:T(8,128)(2,1)} %get-tuple-element.275, s32[]{:T(128)S(6)} %select_n.63), kind=kOutput, calls=%fused_computation.5.clone.1 | convolution fusion | flops 677642240 | bytes 5351429 | tf_op jit(solution)/shard_map/while/body/eval_jaxpr/fdr,fre->fde/dot_general | solution.py:35
  14.1 0.6 dynamic_slice.25
  15.4 4.8 %fusion.55 = f32[1,64,10240]{2,1,0:T(8,128)S(1)} fusion(s32[10240]{0:T(1024)S(1)} %bitcast.90, s32[512]{0:T(512)S(1)} %bitcast.88, f32[1,64,10240]{2,1,0:T(8,128)S(1)} %get-tuple-element.264, pred[]{:T(512)S(6)} %compare.3, bf16[1,64,4096]{2,1,0:T(8,128)(2,1)} %get-tuple-element.275, s32[]{:T(128)S(6)} %select_n.63), kind=kOutput, calls=%fused_computation.5.clone.1 | convolution fusion | flops 677642240 | bytes 5351429 | tf_op jit(solution)/shard_map/while/body/eval_jaxpr/fdr,fre->fde/dot_general | solution.py:35
  20.2 0.6 dynamic_slice.25
  21.5 4.8 %fusion.55 = f32[1,64,10240]{2,1,0:T(8,128)S(1)} fusion(s32[10240]{0:T(1024)S(1)} %bitcast.90, s32[512]{0:T(512)S(1)} %bitcast.88, f32[1,64,10240]{2,1,0:T(8,128)S(1)} %get-tuple-element.264, pred[]{:T(512)S(6)} %compare.3, bf16[1,64,4096]{2,1,0:T(8,128)(2,1)} %get-tuple-element.275, s32[]{:T(128)S(6)} %select_n.63), kind=kOutput, calls=%fused_computation.5.clone.1 | convolution fusion | flops 677642240 | bytes 5351429 | tf_op jit(solution)/shard_map/while/body/eval_jaxpr/fdr,fre->fde/dot_general | solution.py:35
  26.3 0.6 dynamic_slice.25
  27.5 4.8 %fusion.55 = f32[1,64,10240]{2,1,0:T(8,128)S(1)} fusion(s32[10240]{0:T(1024)S(1)} %bitcast.90, s32[512]{0:T(512)S(1)} %bitcast.88, f32[1,64,10240]{2,1,0:T(8,128)S(1)} %get-tuple-element.264, pred[]{:T(512)S(6)} %compare.3, bf16[1,64,4096]{2,1,0:T(8,128)(2,1)} %get-tuple-element.275, s32[]{:T(128)S(6)} %select_n.63), kind=kOutput, calls=%fused_computation.5.clone.1 | convolution fusion | flops 677642240 | bytes 5351429 | tf_op jit(solution)/shard_map/while/body/eval_jaxpr/fdr,fre->fde/dot_general | solution.py:35
  32.4 0.6 dynamic_slice.25
  33.6 4.8 %fusion.55 = f32[1,64,10240]{2,1,0:T(8,128)S(1)} fusion(s32[10240]{0:T(1024)S(1)} %bitcast.90, s32[512]{0:T(512)S(1)} %bitcast.88, f32[1,64,10240]{2,1,0:T(8,128)S(1)} %get-tuple-element.264, pred[]{:T(512)S(6)} %compare.3, bf16[1,64,4096]{2,1,0:T(8,128)(2,1)} %get-tuple-element.275, s32[]{:T(128)S(6)} %select_n.63), kind=kOutput, calls=%fused_computation.5.clone.1 | convolution fusion | flops 677642240 | bytes 5351429 | tf_op jit(solution)/shard_map/while/body/eval_jaxpr/fdr,fre->fde/dot_general | solution.py:35
  38.4 0.6 dynamic_slice.25
  39.7 4.8 %fusion.55 = f32[1,64,10240]{2,1,0:T(8,128)S(1)} fusion(s32[10240]{0:T(1024)S(1)} %bitcast.90, s32[512]{0:T(512)S(1)} %bitcast.88, f32[1,64,10240]{2,1,0:T(8,128)S(1)} %get-tuple-element.264, pred[]{:T(512)S(6)} %compare.3, bf16[1,64,4096]{2,1,0:T(8,128)(2,1)} %get-tuple-element.275, s32[]{:T(128)S(6)} %select_n.63), kind=kOutput, calls=%fused_computation.5.clone.1 | convolution fusion | flops 677642240 | bytes 5351429 | tf_op jit(solution)/shard_map/while/body/eval_jaxpr/fdr,fre->fde/dot_general | solution.py:35
  44.5 0.6 dynamic_slice.25
  45.8 4.8 %fusion.55 = f32[1,64,10240]{2,1,0:T(8,128)S(1)} fusion(s32[10240]{0:T(1024)S(1)} %bitcast.90, s32[512]{0:T(512)S(1)} %bitcast.88, f32[1,64,10240]{2,1,0:T(8,128)S(1)} %get-tuple-element.264, pred[]{:T(512)S(6)} %compare.3, bf16[1,64,4096]{2,1,0:T(8,128)(2,1)} %get-tuple-element.275, s32[]{:T(128)S(6)} %select_n.63), kind=kOutput, calls=%fused_computation.5.clone.1 | convolution fusion | flops 677642240 | bytes 5351429 | tf_op jit(solution)/shard_map/while/body/eval_jaxpr/fdr,fre->fde/dot_general | solution.py:35
  50.6 0.6 dynamic_slice.25
  51.8 4.8 %fusion.55 = f32[1,64,10240]{2,1,0:T(8,128)S(1)} fusion(s32[10240]{0:T(1024)S(1)} %bitcast.90, s32[512]{0:T(512)S(1)} %bitcast.88, f32[1,64,10240]{2,1,0:T(8,128)S(1)} %get-tuple-element.264, pred[]{:T(512)S(6)} %compare.3, bf16[1,64,4096]{2,1,0:T(8,128)(2,1)} %get-tuple-element.275, s32[]{:T(128)S(6)} %select_n.63), kind=kOutput, calls=%fused_computation.5.clone.1 | convolution fusion | flops 677642240 | bytes 5351429 | tf_op jit(solution)/shard_map/while/body/eval_jaxpr/fdr,fre->fde/dot_general | solution.py:35
  56.7 0.1 convert_element_type.41
  56.8 0.2 copy.18
  57.0 0.4 copy-done.1
  57.5 5.2 %fusion.39 = f32[8,1,64,128]{3,2,0,1:T(8,128)} fusion(s32[8,1280]{1,0:T(8,128)S(1)} %bitcast_select_fusion, s32[8,1280]{1,0:T(8,128)S(1)} %bitcast.94, bf16[64,8,1280]{2,1,0:T(8,128)(2,1)S(1)} %bitcast.82), kind=kOutput, calls=%fused_computation.34 | convolution fusion | flops 171704320 | bytes 1654784 | tf_op jit(solution)/shard_map/fdnk,fnkj->nfdj/dot_general | solution.py:50
  62.9 28.1 %all_gather.3 = bf16[1,64,1024]{2,1,0:T(8,128)(2,1)S(1)} all-gather(bf16[1,64,128]{2,1,0:T(8,128)(2,1)S(1)} %copy-done.2), channel_id=1, replica_groups=mesh['rows'=8,'dims'=4] {'rows'}, dimensions={2}, use_global_device_ids=true | all-gather | bytes 147456 | tf_op jit(solution)/shard_map/all_gather | solution.py:55
  91.0 3.1 %fusion.32 = bf16[1,8,8,8,1280]{4,3,2,1,0:T(8,128)(2,1)S(1)} fusion(s32[8,1280]{1,0:T(8,128)S(1)} %bitcast.95, bf16[64,8,128]{2,1,0:T(8,128)(2,1)S(1)} %bitcast.84), kind=kOutput, calls=%fused_computation.27 | convolution fusion | flops 169738240 | bytes 1482752 | tf_op jit(solution)/shard_map/fdnj,fnkj->fdnk/dot_general | solution.py:58
  94.3 38.5 %while.24 = (s32[]{:T(128)}, f32[8,1,64,512]{3,2,1,0:T(8,128)S(1)}, s32[1,1,10240]{2,1,0:T(1,128)S(1)}, s32[8]{0:T(128)S(1)}, bf16[1,1,10240]{2,1,0:T(2,128)(2,1...) while((s32[]{:T(128)}, f32[8,1,64,512]{3,2,1,0:T(8,128)S(1)}, ...), condition=%wide.region_4.5_spmd.clone, body=%wide.region_3.4_spmd.clone.sunk | while | flops 681574912 | bytes 1548423 | solution.py:68
  94.4 0.6 dynamic_slice.23
  95.7 3.4 %fusion.52 = f32[8,1,64,512]{3,2,1,0:T(8,128)S(1)} fusion(f32[8,1,64,512]{3,2,1,0:T(8,128)S(1)} %get-tuple-element.291, s32[]{:T(128)S(6)} %copy.36, bf16[1,64,10240]{2,1,0:T(8,128)(2,1)S(1)} %get-tuple-element.304, s32[10240]{0:T(1024)S(1)} %bitcast.91, s32[512]{0:T(512)S(1)} %bitcast.89, bf16[10240]{0:T(1024)(128)(2,1)S(1)} %reduce.5), kind=kOutput, calls=%fused_computation.20.clone.1 | convolution fusion | flops 681574400 | bytes 1505284 | tf_op jit(solution)/shard_map/while/body/eval_jaxpr/fde,fre->fdr/dot_general | solution.py:66
  99.2 0.6 dynamic_slice.23
  100.5 3.4 %fusion.52 = f32[8,1,64,512]{3,2,1,0:T(8,128)S(1)} fusion(f32[8,1,64,512]{3,2,1,0:T(8,128)S(1)} %get-tuple-element.291, s32[]{:T(128)S(6)} %copy.36, bf16[1,64,10240]{2,1,0:T(8,128)(2,1)S(1)} %get-tuple-element.304, s32[10240]{0:T(1024)S(1)} %bitcast.91, s32[512]{0:T(512)S(1)} %bitcast.89, bf16[10240]{0:T(1024)(128)(2,1)S(1)} %reduce.5), kind=kOutput, calls=%fused_computation.20.clone.1 | convolution fusion | flops 681574400 | bytes 1505284 | tf_op jit(solution)/shard_map/while/body/eval_jaxpr/fde,fre->fdr/dot_general | solution.py:66
  104.0 0.6 dynamic_slice.23
  105.2 0.1 reduce.5
  105.3 3.4 %fusion.52 = f32[8,1,64,512]{3,2,1,0:T(8,128)S(1)} fusion(f32[8,1,64,512]{3,2,1,0:T(8,128)S(1)} %get-tuple-element.291, s32[]{:T(128)S(6)} %copy.36, bf16[1,64,10240]{2,1,0:T(8,128)(2,1)S(1)} %get-tuple-element.304, s32[10240]{0:T(1024)S(1)} %bitcast.91, s32[512]{0:T(512)S(1)} %bitcast.89, bf16[10240]{0:T(1024)(128)(2,1)S(1)} %reduce.5), kind=kOutput, calls=%fused_computation.20.clone.1 | convolution fusion | flops 681574400 | bytes 1505284 | tf_op jit(solution)/shard_map/while/body/eval_jaxpr/fde,fre->fdr/dot_general | solution.py:66
  108.8 0.6 dynamic_slice.23
  110.0 0.1 reduce.5
  110.1 3.4 %fusion.52 = f32[8,1,64,512]{3,2,1,0:T(8,128)S(1)} fusion(f32[8,1,64,512]{3,2,1,0:T(8,128)S(1)} %get-tuple-element.291, s32[]{:T(128)S(6)} %copy.36, bf16[1,64,10240]{2,1,0:T(8,128)(2,1)S(1)} %get-tuple-element.304, s32[10240]{0:T(1024)S(1)} %bitcast.91, s32[512]{0:T(512)S(1)} %bitcast.89, bf16[10240]{0:T(1024)(128)(2,1)S(1)} %reduce.5), kind=kOutput, calls=%fused_computation.20.clone.1 | convolution fusion | flops 681574400 | bytes 1505284 | tf_op jit(solution)/shard_map/while/body/eval_jaxpr/fde,fre->fdr/dot_general | solution.py:66
  113.6 0.6 dynamic_slice.23
  114.8 0.1 reduce.5
  115.0 3.4 %fusion.52 = f32[8,1,64,512]{3,2,1,0:T(8,128)S(1)} fusion(f32[8,1,64,512]{3,2,1,0:T(8,128)S(1)} %get-tuple-element.291, s32[]{:T(128)S(6)} %copy.36, bf16[1,64,10240]{2,1,0:T(8,128)(2,1)S(1)} %get-tuple-element.304, s32[10240]{0:T(1024)S(1)} %bitcast.91, s32[512]{0:T(512)S(1)} %bitcast.89, bf16[10240]{0:T(1024)(128)(2,1)S(1)} %reduce.5), kind=kOutput, calls=%fused_computation.20.clone.1 | convolution fusion | flops 681574400 | bytes 1505284 | tf_op jit(solution)/shard_map/while/body/eval_jaxpr/fde,fre->fdr/dot_general | solution.py:66
  118.4 0.6 dynamic_slice.23
  119.8 3.4 %fusion.52 = f32[8,1,64,512]{3,2,1,0:T(8,128)S(1)} fusion(f32[8,1,64,512]{3,2,1,0:T(8,128)S(1)} %get-tuple-element.291, s32[]{:T(128)S(6)} %copy.36, bf16[1,64,10240]{2,1,0:T(8,128)(2,1)S(1)} %get-tuple-element.304, s32[10240]{0:T(1024)S(1)} %bitcast.91, s32[512]{0:T(512)S(1)} %bitcast.89, bf16[10240]{0:T(1024)(128)(2,1)S(1)} %reduce.5), kind=kOutput, calls=%fused_computation.20.clone.1 | convolution fusion | flops 681574400 | bytes 1505284 | tf_op jit(solution)/shard_map/while/body/eval_jaxpr/fde,fre->fdr/dot_general | solution.py:66
  123.2 0.6 dynamic_slice.23
  124.6 3.4 %fusion.52 = f32[8,1,64,512]{3,2,1,0:T(8,128)S(1)} fusion(f32[8,1,64,512]{3,2,1,0:T(8,128)S(1)} %get-tuple-element.291, s32[]{:T(128)S(6)} %copy.36, bf16[1,64,10240]{2,1,0:T(8,128)(2,1)S(1)} %get-tuple-element.304, s32[10240]{0:T(1024)S(1)} %bitcast.91, s32[512]{0:T(512)S(1)} %bitcast.89, bf16[10240]{0:T(1024)(128)(2,1)S(1)} %reduce.5), kind=kOutput, calls=%fused_computation.20.clone.1 | convolution fusion | flops 681574400 | bytes 1505284 | tf_op jit(solution)/shard_map/while/body/eval_jaxpr/fde,fre->fdr/dot_general | solution.py:66
  128.0 0.6 dynamic_slice.23
  129.4 3.4 %fusion.52 = f32[8,1,64,512]{3,2,1,0:T(8,128)S(1)} fusion(f32[8,1,64,512]{3,2,1,0:T(8,128)S(1)} %get-tuple-element.291, s32[]{:T(128)S(6)} %copy.36, bf16[1,64,10240]{2,1,0:T(8,128)(2,1)S(1)} %get-tuple-element.304, s32[10240]{0:T(1024)S(1)} %bitcast.91, s32[512]{0:T(512)S(1)} %bitcast.89, bf16[10240]{0:T(1024)(128)(2,1)S(1)} %reduce.5), kind=kOutput, calls=%fused_computation.20.clone.1 | convolution fusion | flops 681574400 | bytes 1505284 | tf_op jit(solution)/shard_map/while/body/eval_jaxpr/fde,fre->fdr/dot_general | solution.py:66
  132.8 0.2 multiply_reduce_fusion
  133.1 10.1 %psum.7 = f32[1,4096]{1,0:T(1,128)S(1)} all-reduce(f32[1,4096]{1,0:T(1,128)S(1)} %bitcast.87), channel_id=1, replica_groups=mesh['rows'=8,'dims'=4] {'dims'}, use_global_device_ids=true, to_apply=%region_6.7 | all-reduce | flops 4096 | bytes 32768 | tf_op jit(solution)/shard_map/psum | solution.py:71
  143.2 0.6 fusion.45
  143.9 0.9 subtract_convert_fusion
  (50 shorter events, 1.3 us)
Async XLA Ops:
  7.2 137.7 %reduce-scatter.2.cloned.1.call-start = ((), (), s32[]{:S(2)}) async-start(), calls=%async_computation.1 | async-start | bytes 294912 | tf_op jit(solution)/shard_map/reduce_scatter | solution.py:49
  56.6 0.8 copy-start.1
  56.6 0.8 copy-start.4
  56.7 0.8 copy-start.5
  57.5 5.4 %copy-start.2 = (bf16[1,64,128]{2,1,0:T(8,128)(2,1)S(1)}, bf16[1,64,128]{2,1,0:T(8,128)(2,1)}, u32[]{:S(2)}) copy-start(bf16[1,64,128]{2,1,0:T(8,128)(2,1)} %param.13) | copy-start | bytes 49156
  132.8 10.4 %copy-start.3 = (f32[1,4096]{1,0:T(1,128)S(1)}, f32[1,4096]{1,0:T(1,128)}, u32[]{:S(2)}) copy-start(f32[1,4096]{1,0:T(1,128)} %param.12) | copy-start | bytes 49156
  132.8 11.1 %copy-start = (bf16[1,64,4096]{2,1,0:T(8,128)(2,1)S(1)}, bf16[1,64,4096]{2,1,0:T(8,128)(2,1)}, u32[]{:S(2)}) copy-start(bf16[1,64,4096]{2,1,0:T(8,128)(2,1)} %get-tuple-element.309) | copy-start | bytes 1572868
Sparse Core Ops, SparseCore 0:
  62.8 64.8 reduce-scatter.1
where the time goes:
time: 152 us
  matrix products  73.9 us (49%)
  blocking collectives  38.2 us (25%)
  between operations  14.2 us (9%)
  local copies, waits for them, and re-layouts  11.3 us (7%)
  loops' own time  11 us (7%)
  other arithmetic  3.03 us (2%)
    dot_general x8, matrix products, lookup_block(): jnp.einsum('fdr,fre->fde', table_part, selector, preferred_element_type=j...  38.3 us
    all_gather x1, blocking collectives, shards(): all_grads = lax.all_gather(grad_pooled, 'rows', axis=2, tiled=True)  28.1 us
    dot_general x8, matrix products, gradient_block(): jnp.einsum('fde,fre->fdr', entry_flat, weighted, preferred_element_type=j...  27.4 us
    psum x1, blocking collectives, shards(): norm_total = lax.psum(squares, 'dims')  10.1 us
    dynamic_slice x16, local copies, waits for them, and re-layouts, shards(): lax.scan(lookup_block, jnp.zeros((feat_count, dim_local, entry_count), jn...  9.38 us
    another operation x1, loops' own time, shards(): lax.scan(lookup_block, jnp.zeros((feat_count, dim_local, entry_count), jn...  5.55 us
    another operation x1, loops' own time, shards(): lax.map(gradient_block, jnp.arange(block_count, dtype=jnp.int32))  5.46 us
    dot_general x1, matrix products, shards(): jnp.einsum('fdnk,fnkj->nfdj', picked, onehot, preferred_element_type=jnp....  5.15 us
  transfers between devices with their start and end apart: 1, of which 0 were waited for; matrix products, arithmetic and copies ran while one was open for 25% of the time, Pallas kernels for 0%

commit v1 on v0

--- a/solution.py
+++ b/solution.py
@@ -3,6 +3,7 @@
 import jax.numpy as jnp
 from jax import lax
 from jax.sharding import PartitionSpec as P
+from jax.lax import all_gather
 
 D = 256
 step_size = 0.3
@@ -68,7 +69,7 @@
     grad_blocks = lax.map(gradient_block, jnp.arange(block_count, dtype=jnp.int32))
     row_grad = jnp.moveaxis(grad_blocks, 0, 2).reshape(feat_count, dim_local, row_local)
     squares = jnp.sum(row_grad * row_grad, axis=1)
-    norm_total = lax.psum(squares, "dims")
+    norm_total = all_gather(squares, axis_name="dims").sum(axis=0)
     new_accum = accum + norm_total / D
     new_table = (
         table.astype(jnp.float32) - step_size * row_grad / jnp.sqrt(new_accum)[:, None, :]

time: 152 us -> 148 us (0.974)
  blocking collectives: 38.2 us -> 33.3 us
    psum x1 -> x0, blocking collectives: 10.1 us -> none  [shards(): norm_total = lax.psum(squares, 'dims')]
    all_gather x0 -> x1, blocking collectives: none -> 5.24 us  [shards(): norm_total = all_gather(squares, axis_name='dims').sum(axis=0)]
  transfers between devices with their start and end apart: 1 -> 1, of which waited for: 0 -> 0; matrix products, arithmetic and copies ran while one was open for 25% -> 26% of each run, Pallas kernels for 0% -> 0%
where the time goes in v1:
time: 148 us; the launch traced here: 147 us
  matrix products  73.9 us (50%)
  blocking collectives  33.3 us (22%)
  between operations  14.2 us (10%)
  local copies, waits for them, and re-layouts  11.3 us (8%)
  loops' own time  11 us (7%)
  other arithmetic  3.1 us (2%)
    dot_general x8, matrix products, lookup_block(): jnp.einsum('fdr,fre->fde', table_part, selector, preferred_element_type=j...  38.3 us
    all_gather x1, blocking collectives, shards(): all_grads = lax.all_gather(grad_pooled, 'rows', axis=2, tiled=True)  28.1 us
    dot_general x8, matrix products, gradient_block(): jnp.einsum('fde,fre->fdr', entry_flat, weighted, preferred_element_type=j...  27.4 us
    dynamic_slice x16, local copies, waits for them, and re-layouts, shards(): lax.scan(lookup_block, jnp.zeros((feat_count, dim_local, entry_count), jn...  9.38 us
    another operation x1, loops' own time, shards(): lax.scan(lookup_block, jnp.zeros((feat_count, dim_local, entry_count), jn...  5.55 us
    another operation x1, loops' own time, shards(): lax.map(gradient_block, jnp.arange(block_count, dtype=jnp.int32))  5.46 us
    all_gather x1, blocking collectives, shards(): norm_total = all_gather(squares, axis_name='dims').sum(axis=0)  5.24 us
    dot_general x1, matrix products, shards(): jnp.einsum('fdnk,fnkj->nfdj', picked, onehot, preferred_element_type=jnp....  5.15 us
  transfers between devices with their start and end apart: 1, of which 0 were waited for; matrix products, arithmetic and copies ran while one was open for 26% of the time, Pallas kernels for 0%

profile of v1, /device:TPU:0, one launch (start us, length us, event | category | flops | bytes accessed | tf_op | source)
XLA Modules:
  0.0 146.9 jit_solution(11211626491128527510)
XLA Ops:
  7.2 0.8 reshape_reshape.3
  8.1 48.6 %while.25 = (s32[]{:T(128)}, f32[1,64,10240]{2,1,0:T(8,128)S(1)}, s32[8]{0:T(128)S(1)}, bf16[1,64,4096]{2,1,0:T(8,128)(2,1)}, s32[1,1,10240]{2,1,0:T(1,128)S(1)}...) while((s32[]{:T(128)}, f32[1,64,10240]{2,1,0:T(8,128)S(1)}, s32[8]{0:T(128)S(1)}, ...), condition=%wide.region_1.2_spmd.clone, body=%wide.region_0.1_spmd.clone.sunk | while | flops 677642752 | bytes 5353649 | solution.py:40
  8.1 0.6 dynamic_slice.25
  9.3 4.8 %fusion.55 = f32[1,64,10240]{2,1,0:T(8,128)S(1)} fusion(s32[10240]{0:T(1024)S(1)} %bitcast.87, s32[512]{0:T(512)S(1)} %bitcast.85, f32[1,64,10240]{2,1,0:T(8,128)S(1)} %get-tuple-element.264, pred[]{:T(512)S(6)} %compare.3, bf16[1,64,4096]{2,1,0:T(8,128)(2,1)} %get-tuple-element.275, s32[]{:T(128)S(6)} %select_n.63), kind=kOutput, calls=%fused_computation.5.clone.1 | convolution fusion | flops 677642240 | bytes 5351429 | tf_op jit(solution)/shard_map/while/body/eval_jaxpr/fdr,fre->fde/dot_general | solution.py:36
  14.1 0.6 dynamic_slice.25
  15.4 4.8 %fusion.55 = f32[1,64,10240]{2,1,0:T(8,128)S(1)} fusion(s32[10240]{0:T(1024)S(1)} %bitcast.87, s32[512]{0:T(512)S(1)} %bitcast.85, f32[1,64,10240]{2,1,0:T(8,128)S(1)} %get-tuple-element.264, pred[]{:T(512)S(6)} %compare.3, bf16[1,64,4096]{2,1,0:T(8,128)(2,1)} %get-tuple-element.275, s32[]{:T(128)S(6)} %select_n.63), kind=kOutput, calls=%fused_computation.5.clone.1 | convolution fusion | flops 677642240 | bytes 5351429 | tf_op jit(solution)/shard_map/while/body/eval_jaxpr/fdr,fre->fde/dot_general | solution.py:36
  20.2 0.6 dynamic_slice.25
  21.5 4.8 %fusion.55 = f32[1,64,10240]{2,1,0:T(8,128)S(1)} fusion(s32[10240]{0:T(1024)S(1)} %bitcast.87, s32[512]{0:T(512)S(1)} %bitcast.85, f32[1,64,10240]{2,1,0:T(8,128)S(1)} %get-tuple-element.264, pred[]{:T(512)S(6)} %compare.3, bf16[1,64,4096]{2,1,0:T(8,128)(2,1)} %get-tuple-element.275, s32[]{:T(128)S(6)} %select_n.63), kind=kOutput, calls=%fused_computation.5.clone.1 | convolution fusion | flops 677642240 | bytes 5351429 | tf_op jit(solution)/shard_map/while/body/eval_jaxpr/fdr,fre->fde/dot_general | solution.py:36
  26.3 0.6 dynamic_slice.25
  27.5 4.8 %fusion.55 = f32[1,64,10240]{2,1,0:T(8,128)S(1)} fusion(s32[10240]{0:T(1024)S(1)} %bitcast.87, s32[512]{0:T(512)S(1)} %bitcast.85, f32[1,64,10240]{2,1,0:T(8,128)S(1)} %get-tuple-element.264, pred[]{:T(512)S(6)} %compare.3, bf16[1,64,4096]{2,1,0:T(8,128)(2,1)} %get-tuple-element.275, s32[]{:T(128)S(6)} %select_n.63), kind=kOutput, calls=%fused_computation.5.clone.1 | convolution fusion | flops 677642240 | bytes 5351429 | tf_op jit(solution)/shard_map/while/body/eval_jaxpr/fdr,fre->fde/dot_general | solution.py:36
  32.4 0.6 dynamic_slice.25
  33.6 4.8 %fusion.55 = f32[1,64,10240]{2,1,0:T(8,128)S(1)} fusion(s32[10240]{0:T(1024)S(1)} %bitcast.87, s32[512]{0:T(512)S(1)} %bitcast.85, f32[1,64,10240]{2,1,0:T(8,128)S(1)} %get-tuple-element.264, pred[]{:T(512)S(6)} %compare.3, bf16[1,64,4096]{2,1,0:T(8,128)(2,1)} %get-tuple-element.275, s32[]{:T(128)S(6)} %select_n.63), kind=kOutput, calls=%fused_computation.5.clone.1 | convolution fusion | flops 677642240 | bytes 5351429 | tf_op jit(solution)/shard_map/while/body/eval_jaxpr/fdr,fre->fde/dot_general | solution.py:36
  38.4 0.6 dynamic_slice.25
  39.7 4.8 %fusion.55 = f32[1,64,10240]{2,1,0:T(8,128)S(1)} fusion(s32[10240]{0:T(1024)S(1)} %bitcast.87, s32[512]{0:T(512)S(1)} %bitcast.85, f32[1,64,10240]{2,1,0:T(8,128)S(1)} %get-tuple-element.264, pred[]{:T(512)S(6)} %compare.3, bf16[1,64,4096]{2,1,0:T(8,128)(2,1)} %get-tuple-element.275, s32[]{:T(128)S(6)} %select_n.63), kind=kOutput, calls=%fused_computation.5.clone.1 | convolution fusion | flops 677642240 | bytes 5351429 | tf_op jit(solution)/shard_map/while/body/eval_jaxpr/fdr,fre->fde/dot_general | solution.py:36
  44.5 0.6 dynamic_slice.25
  45.8 4.8 %fusion.55 = f32[1,64,10240]{2,1,0:T(8,128)S(1)} fusion(s32[10240]{0:T(1024)S(1)} %bitcast.87, s32[512]{0:T(512)S(1)} %bitcast.85, f32[1,64,10240]{2,1,0:T(8,128)S(1)} %get-tuple-element.264, pred[]{:T(512)S(6)} %compare.3, bf16[1,64,4096]{2,1,0:T(8,128)(2,1)} %get-tuple-element.275, s32[]{:T(128)S(6)} %select_n.63), kind=kOutput, calls=%fused_computation.5.clone.1 | convolution fusion | flops 677642240 | bytes 5351429 | tf_op jit(solution)/shard_map/while/body/eval_jaxpr/fdr,fre->fde/dot_general | solution.py:36
  50.6 0.6 dynamic_slice.25
  51.8 4.8 %fusion.55 = f32[1,64,10240]{2,1,0:T(8,128)S(1)} fusion(s32[10240]{0:T(1024)S(1)} %bitcast.87, s32[512]{0:T(512)S(1)} %bitcast.85, f32[1,64,10240]{2,1,0:T(8,128)S(1)} %get-tuple-element.264, pred[]{:T(512)S(6)} %compare.3, bf16[1,64,4096]{2,1,0:T(8,128)(2,1)} %get-tuple-element.275, s32[]{:T(128)S(6)} %select_n.63), kind=kOutput, calls=%fused_computation.5.clone.1 | convolution fusion | flops 677642240 | bytes 5351429 | tf_op jit(solution)/shard_map/while/body/eval_jaxpr/fdr,fre->fde/dot_general | solution.py:36
  56.7 0.1 convert_element_type.41
  56.8 0.2 copy.22
  57.0 0.4 copy-done.1
  57.5 5.2 %fusion.39 = f32[8,1,64,128]{3,2,0,1:T(8,128)} fusion(s32[8,1280]{1,0:T(8,128)S(1)} %bitcast_select_fusion, s32[8,1280]{1,0:T(8,128)S(1)} %bitcast.91, bf16[64,8,1280]{2,1,0:T(8,128)(2,1)S(1)} %bitcast.80), kind=kOutput, calls=%fused_computation.34 | convolution fusion | flops 171704320 | bytes 1654784 | tf_op jit(solution)/shard_map/fdnk,fnkj->nfdj/dot_general | solution.py:51
  62.9 28.1 %all_gather.9 = bf16[1,64,1024]{2,1,0:T(8,128)(2,1)S(1)} all-gather(bf16[1,64,128]{2,1,0:T(8,128)(2,1)S(1)} %copy-done.2), channel_id=1, replica_groups=mesh['rows'=8,'dims'=4] {'rows'}, dimensions={2}, use_global_device_ids=true | all-gather | bytes 147456 | tf_op jit(solution)/shard_map/all_gather | solution.py:56
  91.0 3.1 %fusion.32 = bf16[1,8,8,8,1280]{4,3,2,1,0:T(8,128)(2,1)S(1)} fusion(s32[8,1280]{1,0:T(8,128)S(1)} %bitcast.92, bf16[64,8,128]{2,1,0:T(8,128)(2,1)S(1)} %bitcast.82), kind=kOutput, calls=%fused_computation.27 | convolution fusion | flops 169738240 | bytes 1482752 | tf_op jit(solution)/shard_map/fdnj,fnkj->fdnk/dot_general | solution.py:59
  94.3 38.5 %while.24 = (s32[]{:T(128)}, f32[8,1,64,512]{3,2,1,0:T(8,128)S(1)}, s32[1,1,10240]{2,1,0:T(1,128)S(1)}, s32[8]{0:T(128)S(1)}, bf16[1,1,10240]{2,1,0:T(2,128)(2,1...) while((s32[]{:T(128)}, f32[8,1,64,512]{3,2,1,0:T(8,128)S(1)}, ...), condition=%wide.region_4.5_spmd.clone, body=%wide.region_3.4_spmd.clone.sunk | while | flops 681574912 | bytes 1548423 | solution.py:69
  94.4 0.6 dynamic_slice.23
  95.7 3.4 %fusion.52 = f32[8,1,64,512]{3,2,1,0:T(8,128)S(1)} fusion(f32[8,1,64,512]{3,2,1,0:T(8,128)S(1)} %get-tuple-element.291, s32[]{:T(128)S(6)} %copy.39, bf16[1,64,10240]{2,1,0:T(8,128)(2,1)S(1)} %get-tuple-element.304, s32[10240]{0:T(1024)S(1)} %bitcast.88, s32[512]{0:T(512)S(1)} %bitcast.86, bf16[10240]{0:T(1024)(128)(2,1)S(1)} %reduce.6), kind=kOutput, calls=%fused_computation.20.clone.1 | convolution fusion | flops 681574400 | bytes 1505284 | tf_op jit(solution)/shard_map/while/body/eval_jaxpr/fde,fre->fdr/dot_general | solution.py:67
  99.2 0.6 dynamic_slice.23
  100.5 3.4 %fusion.52 = f32[8,1,64,512]{3,2,1,0:T(8,128)S(1)} fusion(f32[8,1,64,512]{3,2,1,0:T(8,128)S(1)} %get-tuple-element.291, s32[]{:T(128)S(6)} %copy.39, bf16[1,64,10240]{2,1,0:T(8,128)(2,1)S(1)} %get-tuple-element.304, s32[10240]{0:T(1024)S(1)} %bitcast.88, s32[512]{0:T(512)S(1)} %bitcast.86, bf16[10240]{0:T(1024)(128)(2,1)S(1)} %reduce.6), kind=kOutput, calls=%fused_computation.20.clone.1 | convolution fusion | flops 681574400 | bytes 1505284 | tf_op jit(solution)/shard_map/while/body/eval_jaxpr/fde,fre->fdr/dot_general | solution.py:67
  104.0 0.6 dynamic_slice.23
  105.2 0.1 reduce.6
  105.3 3.4 %fusion.52 = f32[8,1,64,512]{3,2,1,0:T(8,128)S(1)} fusion(f32[8,1,64,512]{3,2,1,0:T(8,128)S(1)} %get-tuple-element.291, s32[]{:T(128)S(6)} %copy.39, bf16[1,64,10240]{2,1,0:T(8,128)(2,1)S(1)} %get-tuple-element.304, s32[10240]{0:T(1024)S(1)} %bitcast.88, s32[512]{0:T(512)S(1)} %bitcast.86, bf16[10240]{0:T(1024)(128)(2,1)S(1)} %reduce.6), kind=kOutput, calls=%fused_computation.20.clone.1 | convolution fusion | flops 681574400 | bytes 1505284 | tf_op jit(solution)/shard_map/while/body/eval_jaxpr/fde,fre->fdr/dot_general | solution.py:67
  108.8 0.6 dynamic_slice.23
  110.0 0.1 reduce.6
  110.1 3.4 %fusion.52 = f32[8,1,64,512]{3,2,1,0:T(8,128)S(1)} fusion(f32[8,1,64,512]{3,2,1,0:T(8,128)S(1)} %get-tuple-element.291, s32[]{:T(128)S(6)} %copy.39, bf16[1,64,10240]{2,1,0:T(8,128)(2,1)S(1)} %get-tuple-element.304, s32[10240]{0:T(1024)S(1)} %bitcast.88, s32[512]{0:T(512)S(1)} %bitcast.86, bf16[10240]{0:T(1024)(128)(2,1)S(1)} %reduce.6), kind=kOutput, calls=%fused_computation.20.clone.1 | convolution fusion | flops 681574400 | bytes 1505284 | tf_op jit(solution)/shard_map/while/body/eval_jaxpr/fde,fre->fdr/dot_general | solution.py:67
  113.6 0.6 dynamic_slice.23
  114.8 0.1 reduce.6
  115.0 3.4 %fusion.52 = f32[8,1,64,512]{3,2,1,0:T(8,128)S(1)} fusion(f32[8,1,64,512]{3,2,1,0:T(8,128)S(1)} %get-tuple-element.291, s32[]{:T(128)S(6)} %copy.39, bf16[1,64,10240]{2,1,0:T(8,128)(2,1)S(1)} %get-tuple-element.304, s32[10240]{0:T(1024)S(1)} %bitcast.88, s32[512]{0:T(512)S(1)} %bitcast.86, bf16[10240]{0:T(1024)(128)(2,1)S(1)} %reduce.6), kind=kOutput, calls=%fused_computation.20.clone.1 | convolution fusion | flops 681574400 | bytes 1505284 | tf_op jit(solution)/shard_map/while/body/eval_jaxpr/fde,fre->fdr/dot_general | solution.py:67
  118.4 0.6 dynamic_slice.23
  119.8 3.4 %fusion.52 = f32[8,1,64,512]{3,2,1,0:T(8,128)S(1)} fusion(f32[8,1,64,512]{3,2,1,0:T(8,128)S(1)} %get-tuple-element.291, s32[]{:T(128)S(6)} %copy.39, bf16[1,64,10240]{2,1,0:T(8,128)(2,1)S(1)} %get-tuple-element.304, s32[10240]{0:T(1024)S(1)} %bitcast.88, s32[512]{0:T(512)S(1)} %bitcast.86, bf16[10240]{0:T(1024)(128)(2,1)S(1)} %reduce.6), kind=kOutput, calls=%fused_computation.20.clone.1 | convolution fusion | flops 681574400 | bytes 1505284 | tf_op jit(solution)/shard_map/while/body/eval_jaxpr/fde,fre->fdr/dot_general | solution.py:67
  123.2 0.6 dynamic_slice.23
  124.6 3.4 %fusion.52 = f32[8,1,64,512]{3,2,1,0:T(8,128)S(1)} fusion(f32[8,1,64,512]{3,2,1,0:T(8,128)S(1)} %get-tuple-element.291, s32[]{:T(128)S(6)} %copy.39, bf16[1,64,10240]{2,1,0:T(8,128)(2,1)S(1)} %get-tuple-element.304, s32[10240]{0:T(1024)S(1)} %bitcast.88, s32[512]{0:T(512)S(1)} %bitcast.86, bf16[10240]{0:T(1024)(128)(2,1)S(1)} %reduce.6), kind=kOutput, calls=%fused_computation.20.clone.1 | convolution fusion | flops 681574400 | bytes 1505284 | tf_op jit(solution)/shard_map/while/body/eval_jaxpr/fde,fre->fdr/dot_general | solution.py:67
  128.0 0.6 dynamic_slice.23
  129.4 3.4 %fusion.52 = f32[8,1,64,512]{3,2,1,0:T(8,128)S(1)} fusion(f32[8,1,64,512]{3,2,1,0:T(8,128)S(1)} %get-tuple-element.291, s32[]{:T(128)S(6)} %copy.39, bf16[1,64,10240]{2,1,0:T(8,128)(2,1)S(1)} %get-tuple-element.304, s32[10240]{0:T(1024)S(1)} %bitcast.88, s32[512]{0:T(512)S(1)} %bitcast.86, bf16[10240]{0:T(1024)(128)(2,1)S(1)} %reduce.6), kind=kOutput, calls=%fused_computation.20.clone.1 | convolution fusion | flops 681574400 | bytes 1505284 | tf_op jit(solution)/shard_map/while/body/eval_jaxpr/fde,fre->fdr/dot_general | solution.py:67
  132.8 0.2 multiply_reduce_fusion
  133.1 5.2 %all_gather.11 = f32[4,1,4096]{2,1,0:T(1,128)S(1)} all-gather(f32[1,1,4096]{2,1,0:T(1,128)S(1)} %all_gather.10), channel_id=1, replica_groups=mesh['rows'=8,'dims'=4] {'dims'}, dimensions={0}, use_global_device_ids=true | all-gather | bytes 81920 | tf_op jit(solution)/shard_map/all_gather | solution.py:72
  138.5 0.6 fusion.45
  139.1 0.9 subtract_convert_fusion
  (52 shorter events, 1.4 us)
Async XLA Ops:
  7.2 132.9 %reduce-scatter.2.cloned.1.call-start = ((), (), s32[]{:S(2)}) async-start(), calls=%async_computation.1 | async-start | bytes 294912 | tf_op jit(solution)/shard_map/reduce_scatter | solution.py:50
  56.6 0.8 copy-start.1
  56.6 0.8 copy-start.4
  56.7 0.8 copy-start.5
  57.5 5.4 %copy-start.2 = (bf16[1,64,128]{2,1,0:T(8,128)(2,1)S(1)}, bf16[1,64,128]{2,1,0:T(8,128)(2,1)}, u32[]{:S(2)}) copy-start(bf16[1,64,128]{2,1,0:T(8,128)(2,1)} %param.13) | copy-start | bytes 49156
  132.8 5.6 %copy-start.3 = (f32[1,4096]{1,0:T(1,128)S(1)}, f32[1,4096]{1,0:T(1,128)}, u32[]{:S(2)}) copy-start(f32[1,4096]{1,0:T(1,128)} %param.12) | copy-start | bytes 49156
  132.8 6.3 %copy-start = (bf16[1,64,4096]{2,1,0:T(8,128)(2,1)S(1)}, bf16[1,64,4096]{2,1,0:T(8,128)(2,1)}, u32[]{:S(2)}) copy-start(bf16[1,64,4096]{2,1,0:T(8,128)(2,1)} %get-tuple-element.309) | copy-start | bytes 1572868
Sparse Core Ops, SparseCore 0:
  62.8 64.8 reduce-scatter.1
